TPU v7x, 128 devices: a whole 4x4x4 slice. The times are simulated.
128 devices in a mesh: seq: 16 (over y, z_lo, core), tp: 8 (over z_hi, x).
Axes of the slice: x: 4, y: 4, z: 4 (z_hi: 2, z_lo: 2; z = z_hi * 2 + z_lo), core: 2. Of those that a mesh axis runs over, the one named last changes fastest.
Arguments:
- tokens: bfloat16 [8192, 2048], P('seq'), may hold values from -6 to 6
- w_zx: float32 [2048, 8192], P(('seq', 'tp')), may hold values from -0.125 to 0.125
- w_dt: float32 [2048, 64], P(('seq', 'tp')), may hold values from -0.26516503 to 0.26516503
- w_bc: float32 [2048, 256], P(('seq', 'tp')), may hold values from -0.125 to 0.125
- conv_x_weight: float32 [4, 4096], P(None, 'tp'), may hold values from -3 to 3
- conv_x_bias: float32 [4096], P('tp'), may hold values from -1.8 to 1.8
- conv_bc_weight: float32 [4, 256], replicated, may hold values from -3 to 3
- conv_bc_bias: float32 [256], replicated, may hold values from -1.8 to 1.8
- dt_bias: float32 [64], P('tp'), may hold values from -11 to -2
- a_log: float32 [64], P('tp'), may hold values from 0 to 2.77
- skip: float32 [64], P('tp'), may hold values from 0.5 to 2
- norm_weight: float32 [4096], P('tp'), may hold values from 0.1 to 1.9
- w_out: float32 [4096, 2048], P('tp', 'seq'), may hold values from -0.09375 to 0.09375
- lengths: int32 [8], replicated, may hold values from 1 to 4096, 8192 in all
- request_group: int32 [32], replicated, may hold values from 0 to 31
Outputs:
- mixed: bfloat16 [8192, 2048], P(('seq', 'tp'))
- request_states: float32 [32, 64, 64, 128], P('seq', 'tp')
Inputs may be any that keep to these rules, and one draw needn't show every extreme that they name: 8 prompts packed end to end in this order; the lengths sum to 8192 and the longest is exactly 4096.
All inputs are finite; a program needn't handle non-finite values.
Results may differ from a plain program's by a relative error of at most 0.011.
Values may be sent and summed in bfloat16 or wider, within the bound.
A program may use at most 128 MiB of HBM per device.

v0:
```python
import jax
import jax.numpy as jnp
from jax import lax
from jax.sharding import PartitionSpec as P

INNER = 4096
GROUP = 256
epsilon = 1e-05


def from_behind(x, axis, by):
    count = lax.axis_size(axis)
    pairs = [(i, i + by) for i in range(count) if 0 <= i + by < count]
    return lax.ppermute(x, axis, pairs)


def segment_of(position, lengths):
    prompt_ends = jnp.cumsum(lengths)
    return jnp.sum((position[:, None] >= prompt_ends[None, :]).astype(jnp.int32), axis=1)


def round_up(n, m):
    return (n + m - 1) // m * m


def on_device(
    tokens,
    w_zx,
    w_dt,
    w_bc,
    conv_x_weight,
    conv_x_bias,
    conv_bc_weight,
    conv_bc_bias,
    dt_bias,
    a_log,
    skip,
    norm_weight,
    w_out,
    lengths,
    request_group,
):
    tp_count = lax.axis_size("tp")
    seq_count = lax.axis_size("seq")
    seq_index = lax.axis_index("seq")
    tok_dev = tokens.shape[0]
    local_rows = w_zx.shape[0]
    inner_local = conv_x_weight.shape[1]
    heads_local = dt_bias.shape[0]
    head_width = inner_local // heads_local
    bc_width = conv_bc_weight.shape[1]
    state_width = bc_width // 2
    taps = conv_x_weight.shape[0]
    groups_dev = tok_dev // GROUP
    zx_part = w_zx.astype(jnp.bfloat16).reshape(local_rows, 2, tp_count, inner_local)
    zx_part = zx_part.transpose(0, 2, 1, 3).reshape(local_rows, tp_count, 2 * inner_local)
    bc_part = jnp.broadcast_to(
        w_bc.astype(jnp.bfloat16)[:, None, :], (local_rows, tp_count, bc_width)
    )
    dt_part = w_dt.astype(jnp.bfloat16).reshape(local_rows, tp_count, heads_local)
    used = 2 * inner_local + bc_width + heads_local
    width = round_up(used, 128)
    pad_part = jnp.zeros((local_rows, tp_count, width - used), jnp.bfloat16)
    packed = jnp.concatenate([zx_part, bc_part, dt_part, pad_part], axis=2)
    packed = packed.reshape(local_rows, tp_count * width)
    block = lax.all_to_all(packed, "tp", split_axis=1, concat_axis=0, tiled=True)
    weights = lax.all_gather(block, "seq", axis=0, tiled=True)
    proj = jnp.dot(tokens, weights, preferred_element_type=jnp.float32)
    zx_low = proj[:, : 2 * inner_local].astype(jnp.bfloat16)
    gate_z = zx_low[:, :inner_local]
    x_raw = zx_low[:, inner_local:]
    bc_raw = proj[:, 2 * inner_local : 2 * inner_local + bc_width].astype(jnp.bfloat16)
    dt_pre = proj[:, 2 * inner_local + bc_width : used]
    raw_mix = jnp.concatenate([x_raw, bc_raw], axis=1)
    conv_weight = jnp.concatenate([conv_x_weight, conv_bc_weight], axis=1)
    conv_bias = jnp.concatenate([conv_x_bias, conv_bc_bias], axis=0)
    rim_rows = from_behind(raw_mix[tok_dev - (taps - 1) :], "seq", 1)
    padded = jnp.concatenate([rim_rows, raw_mix], axis=0)
    offset = seq_index * tok_dev
    seg_pad = segment_of(
        offset - (taps - 1) + jnp.arange(tok_dev + taps - 1, dtype=jnp.int32), lengths
    )
    seg_tok = seg_pad[taps - 1 :]
    conv_sum = jnp.zeros((tok_dev, raw_mix.shape[1]), jnp.float32) + conv_bias[None, :]
    for offset_tap in range(taps):
        rows_wide = padded[offset_tap : offset_tap + tok_dev].astype(jnp.float32)
        keep_tap = seg_pad[offset_tap : offset_tap + tok_dev] == seg_tok
        conv_sum = conv_sum + jnp.where(
            keep_tap[:, None], rows_wide * conv_weight[offset_tap][None, :], 0.0
        )
    convolved = jax.nn.silu(conv_sum).astype(jnp.bfloat16)
    inputs = convolved[:, :inner_local].reshape(groups_dev, GROUP, heads_local, head_width)
    b_matrix = convolved[:, inner_local : inner_local + state_width].reshape(
        groups_dev, GROUP, state_width
    )
    c_matrix = convolved[:, inner_local + state_width :].reshape(groups_dev, GROUP, state_width)
    step_size = jax.nn.softplus(dt_pre + dt_bias[None, :]).reshape(groups_dev, GROUP, heads_local)
    step_heads = step_size.transpose(0, 2, 1)
    decay_rate = -jnp.exp(a_log)
    cumul_heads = jnp.cumsum(step_size * decay_rate[None, None, :], axis=1).transpose(0, 2, 1)
    segments = seg_tok.reshape(groups_dev, GROUP)
    seg_before = segment_of(offset + jnp.arange(groups_dev, dtype=jnp.int32) * GROUP - 1, lengths)
    within = jnp.arange(GROUP, dtype=jnp.int32)
    same_prompt = (segments[:, :, None] == segments[:, None, :]) & (
        within[:, None] >= within[None, :]
    )[None]
    log_decay = cumul_heads[:, :, :, None] - cumul_heads[:, :, None, :]
    decay_matrix = jnp.where(
        same_prompt[:, None], jnp.exp(jnp.where(same_prompt[:, None], log_decay, 0.0)), 0.0
    )
    scores = jnp.einsum("cin,cjn->cij", c_matrix, b_matrix, preferred_element_type=jnp.float32)
    mix_weights = (decay_matrix * scores[:, None] * step_heads[:, :, None, :]).astype(jnp.bfloat16)
    diag_out = jnp.einsum(
        "chij,cjhp->cihp", mix_weights, inputs, preferred_element_type=jnp.float32
    )
    last_segment = segments[:, -1]
    tail_weight = (
        jnp.where(
            (segments == last_segment[:, None])[:, None, :],
            jnp.exp(cumul_heads[:, :, -1:] - cumul_heads),
            0.0,
        )
        * step_heads
    )
    b_weighted = (b_matrix.astype(jnp.float32)[:, None] * tail_weight[:, :, :, None]).astype(
        jnp.bfloat16
    )
    contrib = jnp.einsum("cjhp,chjn->chpn", inputs, b_weighted, preferred_element_type=jnp.float32)
    pass_gate = jnp.where(
        (last_segment == seg_before)[:, None], jnp.exp(cumul_heads[:, :, -1]), 0.0
    )

    def local_step(carry_state, group_item):
        factor, source = group_item
        next_state = factor[:, None, None] * carry_state + source
        return (next_state, (carry_state, next_state))

    zero_state = jnp.zeros((heads_local, head_width, state_width), jnp.float32)
    _, (local_in, local_end) = lax.scan(local_step, zero_state, (pass_gate, contrib))
    through_group = jnp.cumprod(pass_gate, axis=0)
    before_group = jnp.concatenate(
        [jnp.ones((1, heads_local), jnp.float32), through_group[:-1]], axis=0
    )
    gate_hi = through_group.astype(jnp.bfloat16)
    gate_lo = (through_group - gate_hi.astype(jnp.float32)).astype(jnp.bfloat16)
    extra = jnp.zeros((groups_dev, heads_local, 8, state_width), jnp.bfloat16)
    extra = extra.at[:, :, 0, :].set(
        jnp.broadcast_to(gate_hi[:, :, None], gate_hi.shape + (state_width,))
    )
    extra = extra.at[:, :, 1, :].set(
        jnp.broadcast_to(gate_lo[:, :, None], gate_lo.shape + (state_width,))
    )
    sendable = jnp.concatenate([local_end.astype(jnp.bfloat16), extra], axis=2)
    every = lax.all_gather(sendable, "seq", axis=0, tiled=False)
    every_end = every[:, :, :, :head_width].astype(jnp.float32)
    every_gate = every[:, :, :, head_width, 0].astype(jnp.float32) + every[
        :, :, :, head_width + 1, 0
    ].astype(jnp.float32)
    dev_gate = every_gate[:, -1]
    dev_ids = jnp.arange(seq_count, dtype=jnp.int32)

    def carry_weights(k):
        between = (dev_ids[:, None] < dev_ids[None, :]) & (dev_ids[None, :] < k)
        factors = jnp.where(between[:, :, None], dev_gate[None, :, :], 1.0)
        return jnp.where((dev_ids < k)[:, None], jnp.prod(factors, axis=1), 0.0)

    own_weights = carry_weights(seq_index)
    slot_ids = jnp.arange(groups_dev, dtype=jnp.int32)
    last_slot = (slot_ids == groups_dev - 1).astype(jnp.float32)
    own_coef = own_weights[:, None, :] * last_slot[None, :, None]
    carried = jnp.einsum(
        "jch,jchpn->hpn",
        own_coef,
        every_end,
        precision=lax.Precision.HIGHEST,
        preferred_element_type=jnp.float32,
    )
    group_in = before_group[:, :, None, None] * carried[None] + local_in
    state_low = group_in.astype(jnp.bfloat16)
    carry_keep = jnp.where((segments == seg_before[:, None])[:, None, :], jnp.exp(cumul_heads), 0.0)
    carry_out = jnp.einsum(
        "cin,chpn->cihp", c_matrix, state_low, preferred_element_type=jnp.float32
    )
    carry_out = carry_out * carry_keep.transpose(0, 2, 1)[:, :, :, None]
    y_local = diag_out + carry_out + skip[None, None, :, None] * inputs.astype(jnp.float32)
    y_local = y_local.reshape(tok_dev, inner_local)
    gated = y_local * jax.nn.silu(gate_z.astype(jnp.float32))
    square_sum = jnp.sum(gated * gated, axis=1)
    scaled = (gated * norm_weight[None, :]).astype(jnp.bfloat16)
    out_shard = w_out.astype(jnp.bfloat16)
    out_block = lax.all_gather(out_shard, "seq", axis=1, tiled=True)
    partial = jnp.dot(scaled, out_block, preferred_element_type=jnp.float32)
    side = jnp.zeros((tok_dev, 128), jnp.float32).at[:, 0].set(square_sum)
    summed = lax.psum_scatter(
        jnp.concatenate([partial, side], axis=1), "tp", scatter_dimension=0, tiled=True
    )
    d_model = out_block.shape[1]
    mean_square = summed[:, d_model] / INNER
    mixed = (summed[:, :d_model] * lax.rsqrt(mean_square + epsilon)[:, None]).astype(jnp.bfloat16)
    req_dev = request_group.shape[0] // seq_count
    mine = lax.dynamic_slice_in_dim(request_group, seq_index * req_dev, req_dev)
    req_k = mine // groups_dev
    req_c = mine % groups_dev
    req_w = jax.vmap(carry_weights)(req_k)
    req_gate = every_gate[req_k, req_c]
    coef = req_gate[:, None, None, :] * req_w[:, :, None, :] * last_slot[None, None, :, None]
    hit = (dev_ids[None, :, None] == req_k[:, None, None]) & (
        slot_ids[None, None, :] == req_c[:, None, None]
    )
    coef = coef + hit[:, :, :, None].astype(jnp.float32)
    request_states = jnp.einsum(
        "rjch,jchpn->rhpn",
        coef,
        every_end,
        precision=lax.Precision.HIGHEST,
        preferred_element_type=jnp.float32,
    )
    return (mixed.astype(jnp.bfloat16), request_states)


def solution(mesh):
    return jax.shard_map(
        on_device,
        mesh=mesh,
        in_specs=(
            P("seq", None),
            P(("seq", "tp"), None),
            P(("seq", "tp"), None),
            P(("seq", "tp"), None),
            P(None, "tp"),
            P("tp"),
            P(),
            P(),
            P("tp"),
            P("tp"),
            P("tp"),
            P("tp"),
            P("tp", "seq"),
            P(),
            P(),
        ),
        out_specs=(P(("seq", "tp"), None), P("seq", "tp", None, None)),
        check_vma=False,
    )
```

profile of v0, /device:TPU:0, one launch (start us, length us, event | category | flops | bytes accessed | tf_op | source)
XLA Modules:
  0.0 278.6 jit_solution(9809869660556258186)
XLA Ops:
  7.3 1.2 convert_element_type.121
  9.3 17.5 %all_to_all.16 = bf16[16,8,1408]{2,0,1:T(8,128)(2,1)} all-to-all(bf16[16,8,1408]{2,0,1:T(8,128)(2,1)S(1)} %concatenate.34), channel_id=1, replica_groups=mesh['seq'=16,'tp'=8] {'tp'}, dimensions={1} | all-to-all | bytes 720896 | tf_op jit(solution)/shard_map/all_to_all | solution.py:66
  30.0 35.2 %all-gather.5.cloned.1.call-done = bf16[2048,1408]{1,0:T(8,128)(2,1)} async-done(((bf16[128,1408]{1,0:T(8,128)(2,1)}), bf16[2048,1408]{1,0:T(8,128)(2,1)}) %all-gather.5.cloned.1.call-update) | async-done | bytes 5767184 | tf_op jit(solution)/shard_map/all_gather | solution.py:67
  65.2 6.9 %fusion.59 = (bf16[512,1408]{0,1:T(8,128)(2,1)}, f32[512,1408]{0,1:T(8,128)S(1)}) fusion(bf16[2048,1408]{1,0:T(8,128)(2,1)} %all-gather.5.cloned.1.call-done, bf16[512,2048]{1,0:T(8,128)(2,1)S(1)} %copy-done), kind=kOutput, calls=%fused_computation.139 | convolution fusion | flops 2953510912 | bytes 12189696 | tf_op jit(solution)/shard_map/dot_general | solution.py:68
  72.3 1.1 reduce-window.19
  74.5 1.0 slice.194
  75.6 2.2 collective-permute-start
  79.1 1.2 slice.195
  81.7 1.4 scatter.11
  83.1 2.9 %multiply_convert_fusion.3 = bf16[512,768]{0,1:T(8,128)(2,1)S(1)} fusion(bf16[512,768]{0,1:T(8,128)(2,1)S(1)} %slice.195, bf16[3,768]{0,1:T(8,128)(2,1)S(1)} %collective-permute-done, f32[768]{0:T(1024)} %get-tuple-element.107, f32[768]{0:T(1024)} %get-tuple-element.108, f32[768]{0:T(1024)} %get-tuple-element.109, f32[768]{0:T(1024)} %get-tuple-element.106, ...), kind=kLoop, calls=%fused_computation.22 | loop fusion | flops 11403264 | bytes 1594368 | tf_op jit(solution)/shard_map/convert_element_type | solution.py:91
  86.8 0.9 reshape.461
  88.6 2.0 fusion.22
  90.5 5.0 %while.18 = (s32[]{:T(128)}, f32[8,64,128]{2,1,0:T(8,128)S(1)}, f32[2,8,64,128]{3,2,1,0:T(8,128)}, bf16[2,8,64,128]{3,2,1,0:T(8,128)(2,1)}, f32[2,8]{1,0:T(2,128...) while((s32[]{:T(128)}, f32[8,64,128]{2,1,0:T(8,128)S(1)}, ...), condition=%wide.region_7.8_spmd.clone, body=%wide.region_6.7_spmd.clone.sunk | while | flops 196611 | bytes 1311907 | solution.py:139
  90.6 1.2 fusion.65
  91.7 1.3 bitcast_dynamic-update-slice_fusion.3
  93.0 1.1 fusion.65
  94.2 1.3 bitcast_dynamic-update-slice_fusion.3
  95.5 1.7 pad_maximum_fusion.1
  97.3 1.6 convert_element_type.144
  101.3 1.2 fusion.34
  102.5 2.5 fusion.12
  105.1 31.7 %all-gather.9.cloned.1.call-done = bf16[32,8,72,128]{3,2,1,0:T(8,128)(2,1)} async-done(((bf16[2,8,72,128]{3,2,1,0:T(8,128)(2,1)}), bf16[32,8,72,128]{3,2,1,0:T(8,128)(2,1)}) %all-gather.9.cloned.1.call-update) | async-done | bytes 4718608 | tf_op jit(solution)/shard_map/all_gather | solution.py:154
  136.7 5.8 %slice.215 = bf16[16,2,8,64,128]{4,3,2,1,0:T(8,128)(2,1)} slice(bf16[16,2,8,72,128]{4,3,2,1,0:T(8,128)(2,1)} %bitcast.91), slice={[0:16], [0:2], [0:8], [0:64], [0:128]} | slice | bytes 8388608 | tf_op jit(solution)/shard_map/slice | solution.py:155
  142.5 1.5 fusion.57
  145.0 6.3 %fusion.3 = f32[8,1,64,128,1]{3,1,4,2,0:T(1,128)S(1)} fusion(f32[16,2,8,1,1]{0,3,1,4,2:T(1,128)S(1)} %copy.133, bf16[16,2,8,64,128]{4,3,2,1,0:T(8,128)(2,1)} %slice.215), kind=kOutput, calls=%fused_computation.11 | convolution fusion | flops 25165824 | bytes 4457472 | tf_op jit(solution)/shard_map/jch,jchpn->hpn/dot_general | solution.py:171
  152.6 1.4 multiply_reduce_fusion
  154.7 21.8 %all-gather.7.cloned.1.call-done = bf16[512,2048]{1,0:T(8,128)(2,1)} async-done(((bf16[512,128]{1,0:T(8,128)(2,1)}), bf16[512,2048]{1,0:T(8,128)(2,1)}) %all-gather.7.cloned.1.call-update) | async-done | bytes 2097168 | tf_op jit(solution)/shard_map/all_gather | solution.py:191
  176.5 3.2 %fusion.27 = f32[512,2048]{1,0:T(8,128)S(1)} fusion(bf16[512,2048]{1,0:T(8,128)(2,1)} %all-gather.7.cloned.1.call-done, f32[512]{0:T(512)S(1)} %copy-done.18, f32[512,512]{0,1:T(8,128)S(1)} %bitcast.94, bf16[512,1408]{0,1:T(8,128)(2,1)} %get-tuple-element.143), kind=kOutput, calls=%fused_computation.46 | convolution fusion | flops 1075838976 | bytes 7866368 | tf_op jit(solution)/shard_map/dot_general | solution.py:192
  179.7 2.4 select_maximum_fusion
  184.4 5.8 %fusion.15 = f32[2,8,64,128]{3,0,2,1:T(2,128)S(1)} fusion(bf16[16,2,8,64,128]{4,3,2,1,0:T(8,128)(2,1)} %slice.215, f32[2,16,2]{1,0,2:T(2,128)S(1)} %and_convert_fusion, f32[2,16,8]{1,0,2:T(2,128)S(1)} %copy.130, f32[2]{0:T(128)S(1)} %compare_convert_fusion), kind=kOutput, calls=%fused_computation.31 | convolution fusion | flops 50332672 | bytes 4719880 | tf_op jit(solution)/shard_map/rjch,jchpn->rhpn/dot_general | solution.py:211
  191.1 78.3 %reduce-scatter.2.cloned.1.call-done = f32[64,2176]{1,0:T(8,128)} async-done(((f32[512,2176]{1,0:T(8,128)}), f32[64,2176]{1,0:T(8,128)}) %reduce-scatter.2.cloned.1.call-update) | async-done | bytes 557072 | tf_op jit(solution)/shard_map/reduce_scatter | solution.py:194
  270.2 1.9 fusion.28
  (133 shorter events, 19.0 us)
Async XLA Ops:
  7.2 58.1 %copy-start = (bf16[512,2048]{1,0:T(8,128)(2,1)S(1)}, bf16[512,2048]{1,0:T(8,128)(2,1)}, u32[]{:S(2)}) copy-start(bf16[512,2048]{1,0:T(8,128)(2,1)} %param.23) | copy-start | bytes 6291460
  7.2 1.8 copy-start.7
  7.2 1.8 copy-start.8
  7.2 19.7 %copy-start.19 = (s32[8]{0:T(128)S(1)}, s32[8]{0:T(128)}, u32[]{:S(2)}) copy-start(s32[8]{0:T(128)} %param.36) | copy-start | bytes 100
  7.2 20.5 %copy-start.9 = (f32[4,512]{1,0:T(4,128)S(1)}, f32[4,512]{1,0:T(4,128)}, u32[]{:S(2)}) copy-start(f32[4,512]{1,0:T(4,128)} %param.27) | copy-start | bytes 24580
  7.2 20.6 %copy-start.10 = (f32[4,256]{1,0:T(4,128)S(1)}, f32[4,256]{1,0:T(4,128)}, u32[]{:S(2)}) copy-start(f32[4,256]{1,0:T(4,128)} %param.29) | copy-start | bytes 12292
  7.2 20.6 %copy-start.13 = (f32[512]{0:T(512)S(1)}, f32[512]{0:T(512)}, u32[]{:S(2)}) copy-start(f32[512]{0:T(512)} %param.28) | copy-start | bytes 6148
  7.2 20.6 %copy-start.14 = (f32[256]{0:T(256)S(1)}, f32[256]{0:T(256)}, u32[]{:S(2)}) copy-start(f32[256]{0:T(256)} %param.30) | copy-start | bytes 3076
  7.3 22.0 %copy-start.20 = (f32[8]{0:T(128)S(1)}, f32[8]{0:T(128)}, u32[]{:S(2)}) copy-start(f32[8]{0:T(128)} %param.32) | copy-start | bytes 100
  7.3 58.0 %all-gather.5.cloned.1.call-start = ((), (), s32[]{:S(2)}) async-start(), calls=%async_computation.2 | async-start | bytes 6127616 | tf_op jit(solution)/shard_map/all_gather | solution.py:67
  26.8 109.9 %all-gather.9.cloned.1.call-start = ((), (), s32[]{:S(2)}) async-start(), calls=%async_computation.5 | async-start | bytes 5013504 | tf_op jit(solution)/shard_map/all_gather | solution.py:154
  27.3 44.9 %copy-start.6 = (s32[2,256]{1,0:T(2,128)}, s32[2,256]{1,0:T(2,128)S(1)}, u32[]{:S(2)}) copy-start(s32[2,256]{1,0:T(2,128)S(1)} %eq.111) | copy-start | bytes 6148
  30.0 42.2 %copy-start.15 = (f32[8]{0:T(128)S(1)}, f32[8]{0:T(128)}, u32[]{:S(2)}) copy-start(f32[8]{0:T(128)} %param.31) | copy-start | bytes 100
  74.3 4.2 %copy-start.3 = (f32[2,8,256]{2,1,0:T(8,128)}, f32[2,8,256]{2,1,0:T(8,128)S(1)}, u32[]{:S(2)}) copy-start(f32[2,8,256]{2,1,0:T(8,128)S(1)} %get-tuple-element.130) | copy-start | bytes 49156
  75.6 7.5 %collective-permute-start = (bf16[3,768]{0,1:T(8,128)(2,1)S(1)}, bf16[3,768]{0,1:T(8,128)(2,1)S(1)}, u32[]{:S(2)}, u32[]{:S(2)}) collective-permute-start(bf16[3,768]{0,1:T(8,128)(2,1)S(1)} %slice.194), channel_id=1, source_target_pairs={{0,8},{8,16},{16,24},{24,32},{32,40},{40,48},{48,56},{56,64},{64,7... | collective-permute-start | bytes 13832 | tf_op jit(solution)/shard_map/ppermute | solution.py:14
  77.8 0.7 copy-start.12
  78.5 0.6 copy-start.11
  95.5 7.0 %copy-start.4 = (f32[2,8,256]{2,1,0:T(8,128)S(1)}, f32[2,8,256]{2,1,0:T(8,128)}, u32[]{:S(2)}) copy-start(f32[2,8,256]{2,1,0:T(8,128)} %copy-done.3) | copy-start | bytes 49156
  97.3 79.2 %all-gather.7.cloned.1.call-start = ((), (), s32[]{:S(2)}) async-start(), calls=%async_computation.3 | async-start | bytes 2228224 | tf_op jit(solution)/shard_map/all_gather | solution.py:191
  99.0 170.4 %reduce-scatter.2.cloned.1.call-start = ((), (), s32[]{:S(2)}) async-start(), calls=%async_computation.4 | async-start | bytes 5013504 | tf_op jit(solution)/shard_map/reduce_scatter | solution.py:194
  145.0 6.3 %copy-start.1 = (f32[2,256,8,64]{1,3,2,0:T(8,128)S(1)}, f32[2,256,8,64]{1,3,2,0:T(8,128)}, u32[]{:S(2)}) copy-start(f32[2,256,8,64]{1,3,2,0:T(8,128)} %fusion.12) | copy-start | bytes 3145732
  145.0 6.3 %copy-start.2 = (f32[2,8,64,128]{3,2,1,0:T(8,128)S(1)}, f32[2,8,64,128]{3,2,1,0:T(8,128)}, u32[]{:S(2)}) copy-start(f32[2,8,64,128]{3,2,1,0:T(8,128)} %get-tuple-element.72) | copy-start | bytes 1572868
  145.0 6.3 %copy-start.5 = (f32[2,256,8]{1,2,0:T(8,128)S(1)}, f32[2,256,8]{1,2,0:T(8,128)}, u32[]{:S(2)}) copy-start(f32[2,256,8]{1,2,0:T(8,128)} %get-tuple-element.129) | copy-start | bytes 49156
  145.0 6.3 %copy-start.16 = (f32[8]{0:T(128)S(1)}, f32[8]{0:T(128)}, u32[]{:S(2)}) copy-start(f32[8]{0:T(128)} %param.33) | copy-start | bytes 100
  152.5 24.0 %copy-start.18 = (f32[512]{0:T(512)S(1)}, f32[512]{0:T(512)}, u32[]{:S(2)}) copy-start(f32[512]{0:T(512)} %param.34) | copy-start | bytes 6148
  182.1 0.7 copy-start.17
Sparse Core Ops, SparseCore 0:
  26.9 38.2 all-gather.4
  97.4 39.2 all-gather.8
  138.9 37.5 all-gather.6
  182.2 87.1 reduce-scatter.1
where the time goes:
time: 280 us; the launch traced here: 279 us
  waiting for transfers between devices  167 us (60%)
  matrix products  28.2 us (10%)
  other arithmetic  25.1 us (9%)
  local copies, waits for them, and re-layouts  24.3 us (9%)
  blocking collectives  17.5 us (6%)
  between operations  14.2 us (5%)
    reduce_scatter x1, waiting for transfers between devices, on_device(): lax.psum_scatter(jnp.concatenate([partial, side], axis=1), 'tp', scatter_...  78.3 us
    all_gather x1, waiting for transfers between devices, on_device(): weights = lax.all_gather(block, 'seq', axis=0, tiled=True)  35.2 us
    all_gather x1, waiting for transfers between devices, on_device(): every = lax.all_gather(sendable, 'seq', axis=0, tiled=False)  31.7 us
    all_gather x1, waiting for transfers between devices, on_device(): out_block = lax.all_gather(out_shard, 'seq', axis=1, tiled=True)  21.8 us
    all_to_all x1, blocking collectives, on_device(): lax.all_to_all(packed, 'tp', split_axis=1, concat_axis=0, tiled=True)  17.5 us
    dot_general x1, matrix products, on_device(): proj = jnp.dot(tokens, weights, preferred_element_type=jnp.float32)  6.92 us
    dot_general x1, matrix products, on_device(): jnp.einsum('jch,jchpn->hpn', own_coef, every_end, precision=lax.Precision...  6.27 us
    dot_general x1, matrix products, on_device(): jnp.einsum('rjch,jchpn->rhpn', coef, every_end, precision=lax.Precision.H...  5.76 us
  transfers between devices with their start and end apart: 5, of which 4 were waited for; matrix products, arithmetic and copies ran while one was open for 15% of the time, Pallas kernels for 0%

commit v1 on v0

--- a/solution.py
+++ b/solution.py
@@ -64,7 +64,9 @@
     packed = jnp.concatenate([zx_part, bc_part, dt_part, pad_part], axis=2)
     packed = packed.reshape(local_rows, tp_count * width)
     block = lax.all_to_all(packed, "tp", split_axis=1, concat_axis=0, tiled=True)
-    weights = lax.all_gather(block, "seq", axis=0, tiled=True)
+    weights = jnp.concatenate(
+        lax.all_to_all(jnp.stack([block] * lax.axis_size("seq")), "seq", 0, 0), axis=0
+    )
     proj = jnp.dot(tokens, weights, preferred_element_type=jnp.float32)
     zx_low = proj[:, : 2 * inner_local].astype(jnp.bfloat16)
     gate_z = zx_low[:, :inner_local]

time: 280 us -> 335 us (1.20)
  waiting for transfers between devices: 167 us -> 215 us
  starting transfers between devices: 2.33 us -> 7.03 us
    all_to_all x0 -> x1, waiting for transfers between devices: none -> 78.7 us  [on_device(): lax.all_to_all(jnp.stack([block] * lax.axis_size('seq')), 'seq', 0, 0)]
    all_gather x1 -> x0, waiting for transfers between devices: 35.2 us -> none  [on_device(): weights = lax.all_gather(block, 'seq', axis=0, tiled=True)]
    all_to_all x0 -> x1, starting transfers between devices: none -> 5.22 us  [on_device(): lax.all_to_all(jnp.stack([block] * lax.axis_size('seq')), 'seq', 0, 0)]
    all_gather x1, waiting for transfers between devices: 31.7 us -> 35.9 us  [on_device(): every = lax.all_gather(sendable, 'seq', axis=0, tiled=False)]
  transfers between devices with their start and end apart: 5 -> 5, of which waited for: 4 -> 4; matrix products, arithmetic and copies ran while one was open for 15% -> 12% of each run, Pallas kernels for 0% -> 0%
where the time goes in v1:
time: 335 us; the launch traced here: 334 us
  waiting for transfers between devices  215 us (64%)
  matrix products  28.2 us (8%)
  local copies, waits for them, and re-layouts  27.5 us (8%)
  other arithmetic  25.1 us (7%)
  blocking collectives  17.4 us (5%)
  between operations  14.2 us (4%)
  starting transfers between devices  7.03 us (2%)
    all_to_all x1, waiting for transfers between devices, on_device(): lax.all_to_all(jnp.stack([block] * lax.axis_size('seq')), 'seq', 0, 0)  78.7 us
    reduce_scatter x1, waiting for transfers between devices, on_device(): lax.psum_scatter(jnp.concatenate([partial, side], axis=1), 'tp', scatter_...  78.3 us
    all_gather x1, waiting for transfers between devices, on_device(): every = lax.all_gather(sendable, 'seq', axis=0, tiled=False)  35.9 us
    all_gather x1, waiting for transfers between devices, on_device(): out_block = lax.all_gather(out_shard, 'seq', axis=1, tiled=True)  21.8 us
    all_to_all x1, blocking collectives, on_device(): lax.all_to_all(packed, 'tp', split_axis=1, concat_axis=0, tiled=True)  17.4 us
    dot_general x1, matrix products, on_device(): proj = jnp.dot(tokens, weights, preferred_element_type=jnp.float32)  6.94 us
  transfers between devices with their start and end apart: 5, of which 4 were waited for; matrix products, arithmetic and copies ran while one was open for 12% of the time, Pallas kernels for 0%

profile of v1, /device:TPU:0, one launch (start us, length us, event | category | flops | bytes accessed | tf_op | source)
XLA Modules:
  0.0 334.1 jit_solution(17920812780556188298)
XLA Ops:
  7.2 1.2 convert_element_type.121
  9.3 17.4 %all_to_all.18 = bf16[16,8,1408]{2,0,1:T(8,128)(2,1)S(1)} all-to-all(bf16[16,8,1408]{2,0,1:T(8,128)(2,1)S(1)} %concatenate.34), channel_id=1, replica_groups=mesh['seq'=16,'tp'=8] {'tp'}, dimensions={1} | all-to-all | bytes 720896 | tf_op jit(solution)/shard_map/all_to_all | solution.py:66
  26.6 3.2 stack.5
  29.8 5.2 %all-to-all-start.1 = ((bf16[16,128,1408]{2,1,0:T(8,128)(2,1)}), bf16[16,128,1408]{2,1,0:T(8,128)(2,1)}, u32[]{:S(2)}, u32[]{:S(2)}) async-start(bf16[16,128,1408]{2,1,0:T(8,128)(2,1)} %stack.5), calls=%async_computation.1 | async-start | bytes 11534336 | tf_op jit(solution)/shard_map/all_to_all | solution.py:68
  38.2 78.7 %all-to-all-done.1 = bf16[16,128,1408]{2,1,0:T(8,128)(2,1)} async-done(((bf16[16,128,1408]{2,1,0:T(8,128)(2,1)}), bf16[16,128,1408]{2,1,0:T(8,128)(2,1)}, u32[]{:S(2)}, u32[]{:S(2)}) %all-to-all-start.1) | async-done | bytes 5767200 | tf_op jit(solution)/shard_map/all_to_all | solution.py:68
  116.9 6.9 %fusion.59 = (bf16[512,1408]{0,1:T(8,128)(2,1)}, f32[512,1408]{0,1:T(8,128)S(1)}) fusion(bf16[2048,1408]{1,0:T(8,128)(2,1)} %bitcast.6, bf16[512,2048]{1,0:T(8,128)(2,1)S(1)} %copy-done), kind=kOutput, calls=%fused_computation.139 | convolution fusion | flops 2953510912 | bytes 12189696 | tf_op jit(solution)/shard_map/dot_general | solution.py:70
  124.0 1.1 reduce-window.19
  127.3 1.7 collective-permute-start
  130.4 1.2 slice.195
  132.9 1.4 scatter.11
  134.3 2.9 multiply_convert_fusion.3
  139.8 2.0 fusion.22
  141.8 5.0 %while.18 = (s32[]{:T(128)}, f32[8,64,128]{2,1,0:T(8,128)S(1)}, f32[2,8,64,128]{3,2,1,0:T(8,128)}, bf16[2,8,64,128]{3,2,1,0:T(8,128)(2,1)}, f32[2,8]{1,0:T(2,128...) while((s32[]{:T(128)}, f32[8,64,128]{2,1,0:T(8,128)S(1)}, ...), condition=%wide.region_7.8_spmd.clone, body=%wide.region_6.7_spmd.clone.sunk | while | flops 196611 | bytes 1311907 | solution.py:141
  141.8 1.2 fusion.65
  142.9 1.3 bitcast_dynamic-update-slice_fusion.3
  144.3 1.1 fusion.65
  145.4 1.3 bitcast_dynamic-update-slice_fusion.3
  146.8 1.7 pad_maximum_fusion.1
  148.6 1.6 convert_element_type.144
  152.6 1.2 fusion.34
  153.8 2.5 fusion.12
  156.3 35.9 %all-gather.6.cloned.1.call-done = bf16[32,8,72,128]{3,2,1,0:T(8,128)(2,1)} async-done(((bf16[2,8,72,128]{3,2,1,0:T(8,128)(2,1)}), bf16[32,8,72,128]{3,2,1,0:T(8,128)(2,1)}) %all-gather.6.cloned.1.call-update) | async-done | bytes 4718608 | tf_op jit(solution)/shard_map/all_gather | solution.py:156
  192.2 5.8 %slice.215 = bf16[16,2,8,64,128]{4,3,2,1,0:T(8,128)(2,1)} slice(bf16[16,2,8,72,128]{4,3,2,1,0:T(8,128)(2,1)} %bitcast.92), slice={[0:16], [0:2], [0:8], [0:64], [0:128]} | slice | bytes 8388608 | tf_op jit(solution)/shard_map/slice | solution.py:157
  197.9 1.5 fusion.57
  200.4 6.3 %fusion.3 = f32[8,1,64,128,1]{3,1,4,2,0:T(1,128)S(1)} fusion(f32[16,2,8,1,1]{0,3,1,4,2:T(1,128)S(1)} %copy.133, bf16[16,2,8,64,128]{4,3,2,1,0:T(8,128)(2,1)} %slice.215), kind=kOutput, calls=%fused_computation.11 | convolution fusion | flops 25165824 | bytes 4457472 | tf_op jit(solution)/shard_map/jch,jchpn->hpn/dot_general | solution.py:173
  208.0 1.4 multiply_reduce_fusion
  210.2 21.8 %all-gather.4.cloned.1.call-done = bf16[512,2048]{1,0:T(8,128)(2,1)} async-done(((bf16[512,128]{1,0:T(8,128)(2,1)}), bf16[512,2048]{1,0:T(8,128)(2,1)}) %all-gather.4.cloned.1.call-update) | async-done | bytes 2097168 | tf_op jit(solution)/shard_map/all_gather | solution.py:193
  231.9 3.2 fusion.27
  235.1 2.4 select_maximum_fusion
  239.9 5.8 %fusion.15 = f32[2,8,64,128]{3,0,2,1:T(2,128)S(1)} fusion(bf16[16,2,8,64,128]{4,3,2,1,0:T(8,128)(2,1)} %slice.215, f32[2,16,2]{1,0,2:T(2,128)S(1)} %and_convert_fusion, f32[2,16,8]{1,0,2:T(2,128)S(1)} %copy.130, f32[2]{0:T(128)S(1)} %compare_convert_fusion), kind=kOutput, calls=%fused_computation.31 | convolution fusion | flops 50332672 | bytes 4719880 | tf_op jit(solution)/shard_map/rjch,jchpn->rhpn/dot_general | solution.py:213
  246.5 78.3 %reduce-scatter.2.cloned.1.call-done = f32[64,2176]{1,0:T(8,128)} async-done(((f32[512,2176]{1,0:T(8,128)}), f32[64,2176]{1,0:T(8,128)}) %reduce-scatter.2.cloned.1.call-update) | async-done | bytes 557072 | tf_op jit(solution)/shard_map/reduce_scatter | solution.py:196
  325.7 1.9 fusion.28
  (133 shorter events, 20.9 us)
Async XLA Ops:
  7.2 109.8 %copy-start = (bf16[512,2048]{1,0:T(8,128)(2,1)S(1)}, bf16[512,2048]{1,0:T(8,128)(2,1)}, u32[]{:S(2)}) copy-start(bf16[512,2048]{1,0:T(8,128)(2,1)} %param.23) | copy-start | bytes 6291460
  7.2 1.7 copy-start.7
  7.2 1.7 copy-start.8
  29.8 5.3 %copy-start.19 = (s32[8]{0:T(128)S(1)}, s32[8]{0:T(128)}, u32[]{:S(2)}) copy-start(s32[8]{0:T(128)} %param.36) | copy-start | bytes 100
  29.8 6.2 %copy-start.9 = (f32[4,512]{1,0:T(4,128)S(1)}, f32[4,512]{1,0:T(4,128)}, u32[]{:S(2)}) copy-start(f32[4,512]{1,0:T(4,128)} %param.27) | copy-start | bytes 24580
  29.8 6.2 %copy-start.10 = (f32[4,256]{1,0:T(4,128)S(1)}, f32[4,256]{1,0:T(4,128)}, u32[]{:S(2)}) copy-start(f32[4,256]{1,0:T(4,128)} %param.29) | copy-start | bytes 12292
  29.8 6.2 %copy-start.13 = (f32[512]{0:T(512)S(1)}, f32[512]{0:T(512)}, u32[]{:S(2)}) copy-start(f32[512]{0:T(512)} %param.28) | copy-start | bytes 6148
  29.8 6.2 %copy-start.14 = (f32[256]{0:T(256)S(1)}, f32[256]{0:T(256)}, u32[]{:S(2)}) copy-start(f32[256]{0:T(256)} %param.30) | copy-start | bytes 3076
  29.8 7.6 %copy-start.20 = (f32[8]{0:T(128)S(1)}, f32[8]{0:T(128)}, u32[]{:S(2)}) copy-start(f32[8]{0:T(128)} %param.32) | copy-start | bytes 100
  29.8 87.1 %all-to-all-start.1 = ((bf16[16,128,1408]{2,1,0:T(8,128)(2,1)}), bf16[16,128,1408]{2,1,0:T(8,128)(2,1)}, u32[]{:S(2)}, u32[]{:S(2)}) async-start(bf16[16,128,1408]{2,1,0:T(8,128)(2,1)} %stack.5), calls=%async_computation.1 | async-start | bytes 11534336 | tf_op jit(solution)/shard_map/all_to_all | solution.py:68
  35.0 157.1 %all-gather.6.cloned.1.call-start = ((), (), s32[]{:S(2)}) async-start(), calls=%async_computation.5 | async-start | bytes 5013504 | tf_op jit(solution)/shard_map/all_gather | solution.py:156
  35.5 88.4 %copy-start.6 = (s32[2,256]{1,0:T(2,128)}, s32[2,256]{1,0:T(2,128)S(1)}, u32[]{:S(2)}) copy-start(s32[2,256]{1,0:T(2,128)S(1)} %eq.111) | copy-start | bytes 6148
  116.9 6.9 %copy-start.15 = (f32[8]{0:T(128)S(1)}, f32[8]{0:T(128)}, u32[]{:S(2)}) copy-start(f32[8]{0:T(128)} %param.31) | copy-start | bytes 100
  126.1 3.7 %copy-start.3 = (f32[2,8,256]{2,1,0:T(8,128)}, f32[2,8,256]{2,1,0:T(8,128)S(1)}, u32[]{:S(2)}) copy-start(f32[2,8,256]{2,1,0:T(8,128)S(1)} %get-tuple-element.130) | copy-start | bytes 49156
  127.3 7.0 %collective-permute-start = (bf16[3,768]{0,1:T(8,128)(2,1)S(1)}, bf16[3,768]{0,1:T(8,128)(2,1)S(1)}, u32[]{:S(2)}, u32[]{:S(2)}) collective-permute-start(bf16[3,768]{0,1:T(8,128)(2,1)S(1)} %slice.194), channel_id=1, source_target_pairs={{0,8},{8,16},{16,24},{24,32},{32,40},{40,48},{48,56},{56,64},{64,7... | collective-permute-start | bytes 13832 | tf_op jit(solution)/shard_map/ppermute | solution.py:14
  129.0 0.7 copy-start.12
  129.8 0.6 copy-start.11
  146.8 7.0 %copy-start.4 = (f32[2,8,256]{2,1,0:T(8,128)S(1)}, f32[2,8,256]{2,1,0:T(8,128)}, u32[]{:S(2)}) copy-start(f32[2,8,256]{2,1,0:T(8,128)} %copy-done.3) | copy-start | bytes 49156
  148.5 83.4 %all-gather.4.cloned.1.call-start = ((), (), s32[]{:S(2)}) async-start(), calls=%async_computation.3 | async-start | bytes 2228224 | tf_op jit(solution)/shard_map/all_gather | solution.py:193
  150.2 174.6 %reduce-scatter.2.cloned.1.call-start = ((), (), s32[]{:S(2)}) async-start(), calls=%async_computation.4 | async-start | bytes 5013504 | tf_op jit(solution)/shard_map/reduce_scatter | solution.py:196
  200.4 6.3 %copy-start.1 = (f32[2,256,8,64]{1,3,2,0:T(8,128)S(1)}, f32[2,256,8,64]{1,3,2,0:T(8,128)}, u32[]{:S(2)}) copy-start(f32[2,256,8,64]{1,3,2,0:T(8,128)} %fusion.12) | copy-start | bytes 3145732
  200.4 6.3 %copy-start.2 = (f32[2,8,64,128]{3,2,1,0:T(8,128)S(1)}, f32[2,8,64,128]{3,2,1,0:T(8,128)}, u32[]{:S(2)}) copy-start(f32[2,8,64,128]{3,2,1,0:T(8,128)} %get-tuple-element.72) | copy-start | bytes 1572868
  200.4 6.3 %copy-start.5 = (f32[2,256,8]{1,2,0:T(8,128)S(1)}, f32[2,256,8]{1,2,0:T(8,128)}, u32[]{:S(2)}) copy-start(f32[2,256,8]{1,2,0:T(8,128)} %get-tuple-element.129) | copy-start | bytes 49156
  200.4 6.3 %copy-start.16 = (f32[8]{0:T(128)S(1)}, f32[8]{0:T(128)}, u32[]{:S(2)}) copy-start(f32[8]{0:T(128)} %param.33) | copy-start | bytes 100
  207.9 24.0 %copy-start.18 = (f32[512]{0:T(512)S(1)}, f32[512]{0:T(512)}, u32[]{:S(2)}) copy-start(f32[512]{0:T(512)} %param.34) | copy-start | bytes 6148
  237.5 0.7 copy-start.17
Sparse Core Ops, SparseCore 0:
  148.6 43.4 all-gather.5
  194.4 37.5 all-gather.3
  237.6 87.1 reduce-scatter.1
